TPU v7x, 32 devices: a whole 2x2x4 slice. The times are simulated.
32 devices in a mesh: col: 8 (over z, x), tile: 4 (over y, core).
Axes of the slice: x: 2, y: 2, z: 4, core: 2. Of those that a mesh axis runs over, the one named last changes fastest.
Arguments:
- initial_image: float32 [16384, 1024], P('tile', 'col'), may hold values from -6 to 6
- panels: float32 [8, 256, 16384], P('col', None, 'tile'), may hold values from -0.046875 to 0.046875
- sinogram: float32 [8, 256, 1024], P(None, 'tile', 'col'), may hold values from -6 to 6
- subset_order: int32 [3], replicated, may hold values from 0 to 7
- step_sizes: float32 [3], replicated, may hold values from 0.5 to 1
Outputs:
- final_image: float32 [16384, 1024], P('tile', 'col')
- final_duals: float32 [8, 256, 1024], P(None, 'tile', 'col')
Inputs may be any that keep to these rules, and one draw needn't show every extreme that they name: `subset_order`: repeats may occur.
All inputs are finite; a program needn't handle non-finite values.
Results may differ from a plain program's by a relative error of at most 0.00013.
Values sent between devices are 32-bit elements; how exact they have to be, the bound alone decides.
No kernel may reach another device: no remote copies, remote signals or barrier semaphores. Data moves between devices by JAX's collectives and lax.ppermute only.
A program may use at most 128 MiB of HBM per device.

v0:
```python
import jax
import jax.numpy as jnp
from jax import lax
from jax.sharding import PartitionSpec as P

WIDTH = 512
ITERS = 3
penalty = 0.2
smoothing = 1.0


def shifted(value, axis, by):
    count = lax.axis_size(axis)
    pairs = [(i, i + by) for i in range(count) if 0 <= i + by < count]
    return lax.ppermute(value, axis, pairs)


def broadcast(value, axis, root):
    mine = lax.axis_index(axis) == root
    return lax.psum(jnp.where(mine, value, jnp.zeros_like(value)), axis)


def divergence(estimate, rows_local, tile_index, total_rows):
    channels = estimate.shape[1]
    image_field = estimate.reshape(rows_local, WIDTH, channels)
    row_below = shifted(image_field[0:1], "tile", -1)
    extended = jnp.concatenate([image_field, row_below], axis=0)
    downward = extended[1:] - extended[:-1]
    global_row = tile_index * rows_local + lax.broadcasted_iota(jnp.int32, (rows_local, 1, 1), 0)
    downward = jnp.where(global_row < total_rows - 1, downward, jnp.zeros_like(downward))
    column_zero = jnp.zeros((rows_local, 1, channels), estimate.dtype)
    across = jnp.concatenate([image_field[:, 1:] - image_field[:, :-1], column_zero], axis=1)
    magnitude = jnp.sqrt(across * across + downward * downward + smoothing * smoothing)
    flux_across = across / magnitude
    flux_down = downward / magnitude
    flux_above = shifted(flux_down[rows_local - 1 :], "tile", 1)
    shifted_across = jnp.concatenate([column_zero, flux_across[:, :-1]], axis=1)
    shifted_down = jnp.concatenate([flux_above, flux_down[:-1]], axis=0)
    divergence_field = flux_across - shifted_across + flux_down - shifted_down
    return divergence_field.reshape(estimate.shape)


def per_device(initial_image, panels, sinogram, subset_order, step_sizes):
    dual_step = step_sizes[0]
    primal_step = step_sizes[1]
    extrapolate = step_sizes[2]
    tile_count = lax.axis_size("tile")
    tile_index = lax.axis_index("tile")
    rows_local = initial_image.shape[0] // WIDTH
    total_rows = rows_local * tile_count
    stored = panels.shape[0]
    rays_local = panels.shape[1] // tile_count
    subset_count = sinogram.shape[0]

    def primal(estimate, extrapolated):
        field_div = divergence(estimate, rows_local, tile_index, total_rows)
        return estimate - primal_step * extrapolated + primal_step * penalty * field_div

    estimate = initial_image
    dual_state = jnp.zeros(sinogram.shape, jnp.float32)
    accumulated = jnp.zeros(initial_image.shape, jnp.float32)
    extrapolated = jnp.zeros(initial_image.shape, jnp.float32)
    for iteration in range(ITERS):
        estimate = primal(estimate, extrapolated)
        subset = subset_order[iteration]
        owner_index = subset // stored
        own_panel = lax.dynamic_index_in_dim(panels, subset % stored, 0, keepdims=False)
        operator_panel = broadcast(own_panel, "col", owner_index)
        current = lax.dynamic_index_in_dim(dual_state, subset, 0, keepdims=False)
        measured = lax.dynamic_index_in_dim(sinogram, subset, 0, keepdims=False)

        def partial_rows(first_row, row_count, operator_panel=operator_panel, estimate=estimate):
            return jnp.dot(
                operator_panel,
                estimate,
                precision=lax.Precision.HIGHEST,
                preferred_element_type=jnp.float32,
            )

        forward = lax.psum_scatter(
            partial_rows(jnp.int32(0), rays_local * lax.axis_size("tile")),
            "tile",
            scatter_dimension=0,
            tiled=True,
        )
        updated = (current + dual_step * forward - dual_step * measured) / (1.0 + dual_step)
        change = updated - current

        def add_back(running, received, first_row, operator_panel=operator_panel):
            return lax.dot_general(
                operator_panel,
                received,
                (((0,), (0,)), ((), ())),
                precision=lax.Precision.HIGHEST,
                preferred_element_type=jnp.float32,
            )

        adjoint = add_back(
            jnp.zeros(estimate.shape, jnp.float32),
            lax.all_gather(change, "tile", axis=0, tiled=True),
            jnp.int32(0),
        )
        dual_state = lax.dynamic_update_index_in_dim(dual_state, updated, subset, 0)
        accumulated = accumulated + adjoint
        extrapolated = accumulated + extrapolate * subset_count * adjoint
    final_image = primal(estimate, extrapolated)
    return (final_image, dual_state)


def solution(mesh):
    in_specs = (P("tile", "col"), P("col", None, "tile"), P(None, "tile", "col"), P(), P())
    out_specs = (P("tile", "col"), P(None, "tile", "col"))
    return jax.shard_map(
        per_device, mesh=mesh, in_specs=in_specs, out_specs=out_specs, check_vma=False
    )
```

profile of v0, /device:TPU:0, one launch (start us, length us, event | category | flops | bytes accessed | tf_op | source)
XLA Modules:
  0.0 561.9 jit_solution(9093737235696430673)
XLA Ops:
  10.5 7.2 %select_bitcast_fusion = (f32[256,4096]{1,0:T(8,128)}, f32[256,4096]{1,0:T(8,128)}, f32[256,4096]{1,0:T(8,128)}) fusion(f32[1,256,4096]{2,1,0:T(8,128)} %param.6, pred[]{:T(512)S(6)} %eq.15, pred[]{:T(512)S(6)} %eq.13, pred[]{:T(512)S(6)} %eq.14), kind=kLoop, calls=%fused_computation | loop fusion | flops 3145728 | bytes 16777220 | tf_op jit(solution)/shard_map/jit(_where)/select_n | solution.py:20
  17.7 1.5 copy-done.4
  20.8 1.9 collective-permute-done
  22.7 2.5 fusion.22
  26.6 8.1 %collective-permute-start.1 = (f32[1,512,128]{2,1,0:T(8,128)S(1)}, f32[1,512,128]{2,1,0:T(8,128)S(1)}, u32[]{:S(2)}, u32[]{:S(2)}) collective-permute-start(f32[1,512,128]{2,1,0:T(8,128)S(1)} %slice.155), channel_id=1, source_target_pairs={{0,1},{1,2},{2,3},{4,5},{5,6},{6,7},{8,9},{9,10},{10,11},{12,13},{... | collective-permute-start | bytes 786440 | tf_op jit(solution)/shard_map/ppermute | solution.py:15
  43.6 1.6 slice.156
  45.2 2.9 fusion.11
  49.9 1.9 collective-permute-done.2
  51.9 2.5 fusion.20
  56.2 6.6 %collective-permute-start.3 = (f32[1,512,128]{2,1,0:T(8,128)S(1)}, f32[1,512,128]{2,1,0:T(8,128)S(1)}, u32[]{:S(2)}, u32[]{:S(2)}) collective-permute-start(f32[1,512,128]{2,1,0:T(8,128)S(1)} %slice.161), channel_id=1, source_target_pairs={{0,1},{1,2},{2,3},{4,5},{5,6},{6,7},{8,9},{9,10},{10,11},{12,13},{... | collective-permute-start | bytes 786440 | tf_op jit(solution)/shard_map/ppermute | solution.py:15
  62.9 352.5 %all-reduce.11.cloned.1.call-done = (f32[256,4096]{1,0:T(8,128)}, f32[256,4096]{1,0:T(8,128)}, f32[256,4096]{1,0:T(8,128)}) async-done(((f32[256,4096]{1,0:T(8,128)}, f32[256,4096]{1,0:T(8,128)}, f32[256,4096]{1,0:T(8,128)}), (f32[256,4096]{1,0:T(8,128)}, f32[256,4096]{1,0:T(8,128)}, f32[256,4096]{1,0:T(8,128)})) %all-reduce.11.cloned.1.call-update) | async-done | bytes 12582928 | tf_op jit(solution)/shard_map/psum | solution.py:20
  415.4 5.9 %fusion.31 = f32[256,128]{1,0:T(8,128)} fusion(f32[256,4096]{1,0:T(8,128)} %get-tuple-element.2, f32[4096,128]{1,0:T(8,128)S(1)} %bitcast_add_fusion.2), kind=kOutput, calls=%fused_computation.66 | convolution fusion | flops 1610612736 | bytes 6422528 | tf_op jit(solution)/shard_map/dot_general | solution.py:73
  421.3 5.1 fusion.12
  426.5 13.7 %reduce-scatter.4.cloned.1.call-done = f32[64,128]{1,0:T(8,128)} async-done(((f32[256,128]{1,0:T(8,128)}), f32[64,128]{1,0:T(8,128)}) %reduce-scatter.4.cloned.1.call-update) | async-done | bytes 32784 | tf_op jit(solution)/shard_map/reduce_scatter | solution.py:80
  441.5 5.9 %all_gather.9 = f32[256,128]{1,0:T(8,128)S(1)} all-gather(f32[64,128]{1,0:T(8,128)S(1)} %get-tuple-element.12), channel_id=1, replica_groups=mesh['col'=8,'tile'=4] {'tile'}, dimensions={0}, use_global_device_ids=true | all-gather | bytes 163840 | tf_op jit(solution)/shard_map/all_gather | solution.py:100
  447.4 11.9 %fusion.2 = (f32[4096,128]{1,0:T(8,128)S(1)}, f32[4096,128]{1,0:T(8,128)}) fusion(f32[4096,128]{1,0:T(8,128)S(1)} %bitcast_add_fusion.2, f32[8,512,128]{2,1,0:T(8,128)} %fusion.12, f32[]{:T(128)} %bitcast.8, f32[]{:T(128)} %bitcast, f32[256,4096]{1,0:T(8,128)} %get-tuple-element.2, f32[256,128]{1,0:T(8,128)S(1)} %all_gather.9), kind=kOutput, calls=%fused_computation.6 | convolution fusion | flops 1613234176 | bytes 12713992 | tf_op jit(solution)/shard_map/dot_general | solution.py:90
  460.6 4.1 fusion.32
  466.1 2.6 slice_subtract_fusion.1
  469.0 2.5 fusion.18
  473.4 5.8 %collective-permute-start.5 = (f32[1,512,128]{2,1,0:T(8,128)S(1)}, f32[1,512,128]{2,1,0:T(8,128)S(1)}, u32[]{:S(2)}, u32[]{:S(2)}) collective-permute-start(f32[1,512,128]{2,1,0:T(8,128)S(1)} %slice.167), channel_id=1, source_target_pairs={{0,1},{1,2},{2,3},{4,5},{5,6},{6,7},{8,9},{9,10},{10,11},{12,13},{... | collective-permute-start | bytes 786440 | tf_op jit(solution)/shard_map/ppermute | solution.py:15
  479.2 5.4 reduce-scatter.6.cloned.1.call-done
  485.9 5.6 all_gather.10
  491.5 4.0 fusion.13
  496.8 9.3 %bitcast_add_fusion.1 = (f32[4096,128]{1,0:T(8,128)S(1)}, f32[4096,128]{1,0:T(8,128)}) fusion(f32[8,512,128]{2,1,0:T(8,128)S(1)} %fusion.13, f32[4096,128]{1,0:T(8,128)S(1)} %copy-done.1, f32[]{:T(128)} %bitcast.8, f32[]{:T(128)} %bitcast, f32[4096,128]{1,0:T(8,128)S(1)} %copy-done.14, f32[256,4096]{1,0:T(8,128)S(1)} %copy-done.13, ...), kind=kOutput, calls=%fused_computation.32 | convolution fusion | flops 1613758464 | bytes 14811144 | tf_op jit(solution)/shard_map/dot_general | solution.py:90
  507.5 4.1 fusion.33
  512.9 4.0 slice_subtract_fusion
  516.9 14.6 %reduce-scatter.8.cloned.1.call-done = f32[64,128]{1,0:T(8,128)} async-done(((f32[256,128]{1,0:T(8,128)}), f32[64,128]{1,0:T(8,128)}) %reduce-scatter.8.cloned.1.call-update) | async-done | bytes 32784 | tf_op jit(solution)/shard_map/reduce_scatter | solution.py:80
  532.8 5.6 %all_gather.11 = f32[256,128]{1,0:T(8,128)S(1)} all-gather(f32[64,128]{1,0:T(8,128)S(1)} %get-tuple-element.5), channel_id=1, replica_groups=mesh['col'=8,'tile'=4] {'tile'}, dimensions={0}, use_global_device_ids=true | all-gather | bytes 163840 | tf_op jit(solution)/shard_map/all_gather | solution.py:100
  538.5 2.9 fusion.16
  541.4 2.3 collective-permute-start.7
  543.7 7.1 %fusion.34 = f32[4096,128]{1,0:T(8,128)S(1)} fusion(f32[256,4096]{1,0:T(8,128)S(1)} %copy-done.11, f32[256,128]{1,0:T(8,128)S(1)} %all_gather.11), kind=kOutput, calls=%fused_computation.69 | convolution fusion | flops 1610612736 | bytes 6422528 | tf_op jit(solution)/shard_map/dot_general | solution.py:90
  552.6 2.5 bitcast_add_fusion
  (77 shorter events, 23.5 us)
Async XLA Ops:
  7.2 408.2 %all-reduce.11.cloned.1.call-start = ((), (), s32[]{:S(2)}) async-start(), calls=%async_computation.6 | async-start | bytes 25165824 | tf_op jit(solution)/shard_map/psum | solution.py:20
  17.7 1.6 copy-start.4
  17.7 422.5 %reduce-scatter.4.cloned.1.call-start = ((), (), s32[]{:S(2)}) async-start(), calls=%async_computation.3 | async-start | bytes 163840 | tf_op jit(solution)/shard_map/reduce_scatter | solution.py:80
  19.3 3.4 collective-permute-start
  20.8 17.7 %copy-start.17 = (f32[3]{0:T(128)S(1)}, f32[3]{0:T(128)}, u32[]{:S(2)}) copy-start(f32[3]{0:T(128)} %param.9) | copy-start | bytes 40
  25.2 1.4 copy-start.6
  26.6 18.6 %copy-start.7 = (f32[8,512,128]{2,1,0:T(8,128)S(1)}, f32[8,512,128]{2,1,0:T(8,128)}, u32[]{:S(2)}) copy-start(f32[8,512,128]{2,1,0:T(8,128)} %copy-done.6) | copy-start | bytes 6291460
  26.6 18.6 %collective-permute-start.1 = (f32[1,512,128]{2,1,0:T(8,128)S(1)}, f32[1,512,128]{2,1,0:T(8,128)S(1)}, u32[]{:S(2)}, u32[]{:S(2)}) collective-permute-start(f32[1,512,128]{2,1,0:T(8,128)S(1)} %slice.155), channel_id=1, source_target_pairs={{0,1},{1,2},{2,3},{4,5},{5,6},{6,7},{8,9},{9,10},{10,11},{12,13},{... | collective-permute-start | bytes 786440 | tf_op jit(solution)/shard_map/ppermute | solution.py:15
  45.2 3.0 copy-start.5
  48.4 3.4 collective-permute-start.2
  54.3 1.9 copy-start.8
  56.2 365.1 %collective-permute-start.3 = (f32[1,512,128]{2,1,0:T(8,128)S(1)}, f32[1,512,128]{2,1,0:T(8,128)S(1)}, u32[]{:S(2)}, u32[]{:S(2)}) collective-permute-start(f32[1,512,128]{2,1,0:T(8,128)S(1)} %slice.161), channel_id=1, source_target_pairs={{0,1},{1,2},{2,3},{4,5},{5,6},{6,7},{8,9},{9,10},{10,11},{12,13},{... | collective-permute-start | bytes 786440 | tf_op jit(solution)/shard_map/ppermute | solution.py:15
  421.3 63.3 %reduce-scatter.6.cloned.1.call-start = ((), (), s32[]{:S(2)}) async-start(), calls=%async_computation.4 | async-start | bytes 163840 | tf_op jit(solution)/shard_map/reduce_scatter | solution.py:80
  447.4 13.2 %copy-start.12 = (f32[256,4096]{1,0:T(8,128)S(1)}, f32[256,4096]{1,0:T(8,128)}, u32[]{:S(2)}) copy-start(f32[256,4096]{1,0:T(8,128)} %get-tuple-element.3) | copy-start | bytes 12582916
  459.3 1.3 copy-start
  464.8 66.7 %reduce-scatter.8.cloned.1.call-start = ((), (), s32[]{:S(2)}) async-start(), calls=%async_computation.5 | async-start | bytes 163840 | tf_op jit(solution)/shard_map/reduce_scatter | solution.py:80
  464.8 3.9 collective-permute-start.4
  466.1 2.9 copy-start.1
  471.5 1.9 copy-start.9
  473.4 18.1 %collective-permute-start.5 = (f32[1,512,128]{2,1,0:T(8,128)S(1)}, f32[1,512,128]{2,1,0:T(8,128)S(1)}, u32[]{:S(2)}, u32[]{:S(2)}) collective-permute-start(f32[1,512,128]{2,1,0:T(8,128)S(1)} %slice.167), channel_id=1, source_target_pairs={{0,1},{1,2},{2,3},{4,5},{5,6},{6,7},{8,9},{9,10},{10,11},{12,13},{... | collective-permute-start | bytes 786440 | tf_op jit(solution)/shard_map/ppermute | solution.py:15
  491.5 4.6 copy-start.13
  491.5 5.3 copy-start.14
  496.8 10.7 %copy-start.10 = (f32[256,4096]{1,0:T(8,128)S(1)}, f32[256,4096]{1,0:T(8,128)}, u32[]{:S(2)}) copy-start(f32[256,4096]{1,0:T(8,128)} %get-tuple-element.4) | copy-start | bytes 12582916
  506.1 1.4 copy-start.2
  511.6 26.8 %collective-permute-start.6 = (f32[1,512,128]{2,1,0:T(8,128)S(1)}, f32[1,512,128]{2,1,0:T(8,128)S(1)}, u32[]{:S(2)}, u32[]{:S(2)}) collective-permute-start(f32[1,512,128]{2,1,0:T(8,128)S(1)} %slice_bitcast_fusion), channel_id=1, source_target_pairs={{1,0},{2,1},{3,2},{5,4},{6,5},{7,6},{9,8},{10,9},{11,10},{13,12},{... | collective-permute-start | bytes 786440 | tf_op jit(solution)/shard_map/ppermute | solution.py:15
  512.9 25.5 %copy-start.3 = (f32[4096,128]{1,0:T(8,128)S(1)}, f32[4096,128]{1,0:T(8,128)}, u32[]{:S(2)}) copy-start(f32[4096,128]{1,0:T(8,128)} %copy-done.2) | copy-start | bytes 6291460
  538.5 5.2 copy-start.11
  541.4 9.5 %collective-permute-start.7 = (f32[1,512,128]{2,1,0:T(8,128)S(1)}, f32[1,512,128]{2,1,0:T(8,128)S(1)}, u32[]{:S(2)}, u32[]{:S(2)}) collective-permute-start(f32[1,512,128]{2,1,0:T(8,128)S(1)} %slice.173), channel_id=1, source_target_pairs={{0,1},{1,2},{2,3},{4,5},{5,6},{6,7},{8,9},{9,10},{10,11},{12,13},{... | collective-permute-start | bytes 786440 | tf_op jit(solution)/shard_map/ppermute | solution.py:15
  550.9 0.7 copy-start.16
  550.9 1.7 copy-start.15
Sparse Core Ops, SparseCore 0:
  17.8 397.5 all-reduce.10
  421.4 18.7 reduce-scatter.3
  464.9 19.6 reduce-scatter.5
  511.7 19.6 reduce-scatter.7
where the time goes:
time: 569 us; the launch traced here: 562 us
  waiting for transfers between devices  390 us (69%)
  other arithmetic  43.8 us (8%)
  matrix products  42.4 us (7%)
  starting transfers between devices  28 us (5%)
  between operations  24.4 us (4%)
  blocking collectives  17.1 us (3%)
  local copies, waits for them, and re-layouts  16.1 us (3%)
    psum x1, waiting for transfers between devices, broadcast(): return lax.psum(jnp.where(mine, value, jnp.zeros_like(value)), axis)  352 us
    reduce_scatter x3, waiting for transfers between devices, per_device(): lax.psum_scatter(partial_rows(jnp.int32(0), rays_local * lax.axis_size('t...  33.7 us
    dot_general x3, matrix products, add_back(): lax.dot_general(operator_panel, received, (((0,), (0,)), ((), ())), preci...  28.2 us
    ppermute x8, starting transfers between devices, shifted(): return lax.ppermute(value, axis, pairs)  27.9 us
    all_gather x3, blocking collectives, per_device(): lax.all_gather(change, 'tile', axis=0, tiled=True)  17.1 us
    dot_general x3, matrix products, partial_rows(): jnp.dot(operator_panel, estimate, precision=lax.Precision.HIGHEST, prefer...  14.1 us
    mul x4, other arithmetic, primal(): primal_step * penalty * field_div  12.5 us
  transfers between devices with their start and end apart: 12, of which 6 were waited for; matrix products, arithmetic and copies ran while one was open for 8% of the time, Pallas kernels for 0%

commit v1 on v0

--- a/solution.py
+++ b/solution.py
@@ -17,7 +17,9 @@
 
 def broadcast(value, axis, root):
     mine = lax.axis_index(axis) == root
-    return lax.psum(jnp.where(mine, value, jnp.zeros_like(value)), axis)
+    return jnp.sum(
+        jax.lax.all_gather(jnp.where(mine, value, jnp.zeros_like(value)), axis_name=axis), 0
+    )
 
 
 def divergence(estimate, rows_local, tile_index, total_rows):

time: 569 us -> 2090 us (3.67)
  waiting for transfers between devices: 390 us -> 1870 us
  other arithmetic: 43.8 us -> 87.8 us
    all_gather x0 -> x3, waiting for transfers between devices: none -> 1830 us  [broadcast(): jax.lax.all_gather(jnp.where(mine, value, jnp.zeros_like(value)), axis_na...]
    psum x1 -> x0, waiting for transfers between devices: 352 us -> none  [broadcast(): return lax.psum(jnp.where(mine, value, jnp.zeros_like(value)), axis)]
    reduce_sum x0 -> x3, other arithmetic: none -> 43.8 us  [broadcast(): jnp.sum(jax.lax.all_gather(jnp.where(mine, value, jnp.zeros_like(value)),...]
  transfers between devices with their start and end apart: 12 -> 14, of which waited for: 6 -> 8; matrix products, arithmetic and copies ran while one was open for 8% -> 4% of each run, Pallas kernels for 0% -> 0%
where the time goes in v1:
time: 2090 us; the launch traced here: 2080 us
  waiting for transfers between devices  1870 us (89%)
  other arithmetic  87.8 us (4%)
  matrix products  42.1 us (2%)
  starting transfers between devices  28.1 us (1%)
  between operations  24.5 us (1%)
    all_gather x3, waiting for transfers between devices, broadcast(): jax.lax.all_gather(jnp.where(mine, value, jnp.zeros_like(value)), axis_na...  1830 us
    reduce_sum x3, other arithmetic, broadcast(): jnp.sum(jax.lax.all_gather(jnp.where(mine, value, jnp.zeros_like(value)),...  43.8 us
  transfers between devices with their start and end apart: 14, of which 8 were waited for; matrix products, arithmetic and copies ran while one was open for 4% of the time, Pallas kernels for 0%

profile of v1, /device:TPU:0, one launch (start us, length us, event | category | flops | bytes accessed | tf_op | source)
XLA Modules:
  0.0 2081.1 jit_solution(12999687777444915782)
XLA Ops:
  10.4 7.2 broadcast_select_fusion
  23.5 2.5 fusion.22
  27.4 8.1 collective-permute-start.1
  45.9 2.9 fusion.11
  52.5 2.5 fusion.20
  56.9 6.6 collective-permute-start.3
  63.4 594.8 %all-gather.4.cloned.1.call-done = f32[8,256,4096]{2,1,0:T(8,128)} async-done(((f32[1,256,4096]{2,1,0:T(8,128)}), f32[8,256,4096]{2,1,0:T(8,128)}) %all-gather.4.cloned.1.call-update) | async-done | bytes 33554448 | tf_op jit(solution)/shard_map/all_gather | solution.py:21
  658.2 14.8 reduce_sum.27
  673.0 5.9 fusion.31
  679.0 5.1 fusion.12
  684.1 613.3 %all-gather.6.cloned.1.call-done = f32[8,256,4096]{2,1,0:T(8,128)} async-done(((f32[1,256,4096]{2,1,0:T(8,128)}), f32[8,256,4096]{2,1,0:T(8,128)}) %all-gather.6.cloned.1.call-update) | async-done | bytes 33554448 | tf_op jit(solution)/shard_map/all_gather | solution.py:21
  1297.4 14.9 reduce_sum.28
  1312.3 624.4 %all-gather.8.cloned.1.call-done = f32[8,256,4096]{2,1,0:T(8,128)} async-done(((f32[1,256,4096]{2,1,0:T(8,128)}), f32[8,256,4096]{2,1,0:T(8,128)}) %all-gather.8.cloned.1.call-update) | async-done | bytes 33554448 | tf_op jit(solution)/shard_map/all_gather | solution.py:21
  1936.6 14.1 reduce_sum.29
  1950.7 8.4 reduce-scatter.4.cloned.1.call-done
  1960.6 5.9 all_gather.22
  1966.5 11.7 fusion.2
  1979.5 4.1 fusion.32
  1985.0 2.6 slice_subtract_fusion.1
  1987.8 2.5 fusion.18
  1992.3 5.8 collective-permute-start.5
  1998.1 5.3 reduce-scatter.6.cloned.1.call-done
  2004.9 5.6 all_gather.24
  2010.5 4.0 fusion.13
  2015.7 9.2 bitcast_add_fusion.1
  2026.3 4.1 fusion.33
  2031.8 3.9 slice_subtract_fusion
  2035.7 14.6 reduce-scatter.8.cloned.1.call-done
  2051.8 5.6 all_gather.26
  2057.4 2.9 fusion.16
  2062.7 7.1 fusion.34
  2071.6 2.4 bitcast_add_fusion
  (86 shorter events, 33.9 us)
Async XLA Ops:
  7.2 651.0 %all-gather.4.cloned.1.call-start = ((), (), s32[]{:S(2)}) async-start(), calls=%async_computation.3 | async-start | bytes 37748736 | tf_op jit(solution)/shard_map/all_gather | solution.py:21
  17.7 1279.7 %all-gather.6.cloned.1.call-start = ((), (), s32[]{:S(2)}) async-start(), calls=%async_computation.5 | async-start | bytes 37748736 | tf_op jit(solution)/shard_map/all_gather | solution.py:21
  18.4 1918.2 %all-gather.8.cloned.1.call-start = ((), (), s32[]{:S(2)}) async-start(), calls=%async_computation.7 | async-start | bytes 37748736 | tf_op jit(solution)/shard_map/all_gather | solution.py:21
  18.5 1.6 copy-start.8
  19.2 1939.9 %reduce-scatter.4.cloned.1.call-start = ((), (), s32[]{:S(2)}) async-start(), calls=%async_computation.4 | async-start | bytes 163840 | tf_op jit(solution)/shard_map/reduce_scatter | solution.py:82
  20.1 3.4 collective-permute-start
  21.6 17.6 copy-start.17
  26.0 1.4 copy-start.10
  27.4 18.4 copy-start.11
  27.4 18.4 collective-permute-start.1
  45.8 2.9 copy-start.9
  49.0 3.4 collective-permute-start.2
  54.9 1.9 copy-start.12
  56.9 622.1 %collective-permute-start.3 = (f32[1,512,128]{2,1,0:T(8,128)S(1)}, f32[1,512,128]{2,1,0:T(8,128)S(1)}, u32[]{:S(2)}, u32[]{:S(2)}) collective-permute-start(f32[1,512,128]{2,1,0:T(8,128)S(1)} %slice.161), channel_id=1, source_target_pairs={{0,1},{1,2},{2,3},{4,5},{5,6},{6,7},{8,9},{9,10},{10,11},{12,13},{... | collective-permute-start | bytes 786440 | tf_op jit(solution)/shard_map/ppermute | solution.py:15
  678.9 1324.5 %reduce-scatter.6.cloned.1.call-start = ((), (), s32[]{:S(2)}) async-start(), calls=%async_computation.6 | async-start | bytes 163840 | tf_op jit(solution)/shard_map/reduce_scatter | solution.py:82
  1966.5 13.0 copy-start.6
  1978.2 1.3 copy-start
  1983.6 66.7 %reduce-scatter.8.cloned.1.call-start = ((), (), s32[]{:S(2)}) async-start(), calls=%async_computation.8 | async-start | bytes 163840 | tf_op jit(solution)/shard_map/reduce_scatter | solution.py:82
  1983.7 3.9 collective-permute-start.4
  1985.0 2.9 copy-start.1
  1990.3 1.9 copy-start.13
  1992.3 18.2 collective-permute-start.5
  2010.5 4.6 copy-start.7
  2010.5 5.3 copy-start.14
  2015.7 10.6 copy-start.4
  2025.0 1.4 copy-start.2
  2030.5 27.0 %collective-permute-start.6 = (f32[1,512,128]{2,1,0:T(8,128)S(1)}, f32[1,512,128]{2,1,0:T(8,128)S(1)}, u32[]{:S(2)}, u32[]{:S(2)}) collective-permute-start(f32[1,512,128]{2,1,0:T(8,128)S(1)} %slice_bitcast_fusion), channel_id=1, source_target_pairs={{1,0},{2,1},{3,2},{5,4},{6,5},{7,6},{9,8},{10,9},{11,10},{13,12},{... | collective-permute-start | bytes 786440 | tf_op jit(solution)/shard_map/ppermute | solution.py:15
  2031.8 25.7 %copy-start.3 = (f32[4096,128]{1,0:T(8,128)S(1)}, f32[4096,128]{1,0:T(8,128)}, u32[]{:S(2)}) copy-start(f32[4096,128]{1,0:T(8,128)} %copy-done.2) | copy-start | bytes 6291460
  2057.4 5.2 copy-start.5
  2060.4 9.5 collective-permute-start.7
  2069.9 0.7 copy-start.16
  2069.9 1.7 copy-start.15
Sparse Core Ops, SparseCore 0:
  17.8 640.3 all-gather.3
  659.7 637.6 all-gather.5
  1298.9 637.6 all-gather.7
  1939.5 19.5 reduce-scatter.3
  1983.8 19.6 reduce-scatter.5
  2030.6 19.6 reduce-scatter.7
